TPU v7x, 32 devices: a whole 2x2x4 slice. The times are simulated.
32 devices in a mesh: expert: 8 (over z, y), dp: 4 (over x, core).
Axes of the slice: x: 2, y: 2, z: 4, core: 2. Of those that a mesh axis runs over, the one named last changes fastest.
Arguments:
- tokens_t: bfloat16 [7168, 512], P('expert', 'dp'), may hold values from -6 to 6
- slot_row: int32 [4, 1024], P('dp'), may hold values from -1 to 127, as said below
- slot_gate: float32 [4, 1024], P('dp'), may hold values from 0.2 to 1
- block_hot: int32 [4, 8], P('dp'), may hold values from 0 to 1, as said below
- hot_owner: int32 [1], replicated, may hold values from 0 to 255
- w_in: bfloat16 [4, 2, 2048, 7168], P('dp', None, 'expert'), may hold values from -0.0625 to 0.0625
- w_out: bfloat16 [4, 7168, 2048], P('dp', None, 'expert'), may hold values from -0.125 to 0.125
Outputs:
- mixed_t: bfloat16 [7168, 512], P('expert', 'dp')
Inputs may be any that keep to these rules, and one draw needn't show every extreme that they name: `slot_row`: each source shard fills each of its slots with a token of that shard or leaves it empty; a token may fill several slots. `block_hot`: every expert group runs at least one block of the hot expert and at least one block of its own expert.
All inputs are finite; a program needn't handle non-finite values.
Results may differ from a plain program's by a relative error of at most 0.014.
Values may be sent and summed in bfloat16 or wider, within the bound.
No kernel may reach another device: no remote copies, remote signals or barrier semaphores. Data moves between devices by JAX's collectives and lax.ppermute only.
A program may use at most 192 MiB of HBM per device.

v0:
```python
import jax
import jax.numpy as jnp
from jax import lax
from jax.sharding import PartitionSpec as P

BLOCK = 128


def from_root(value, axis, source):
    kept = jnp.where(lax.axis_index(axis) == source, value, 0).astype(value.dtype)
    return lax.psum(kept, axis)


def local(tokens_t, slot_row, slot_gate, block_hot, hot_owner, w_in, w_out):
    slot_ids = slot_row[0]
    slot_weights = slot_gate[0]
    hot_flags = block_hot[0]
    num_blocks = hot_flags.shape[0]
    tok_local = tokens_t.shape[1]
    feature_rows = tokens_t.shape[0]
    width = w_in.shape[3]
    live_mask = (slot_ids >= 0).astype(tokens_t.dtype)
    row_index = jnp.maximum(slot_ids, 0)
    slot_total = slot_ids.shape[0]
    res_in = w_in[0].reshape(-1, width)
    root_index = hot_owner[0] % lax.axis_size("dp")
    hot_pair = (from_root(w_in, "dp", root_index), from_root(w_out, "dp", root_index))
    hot_in = hot_pair[0][0].reshape(-1, width)
    hot_out_full = hot_pair[1]
    empty_sum = jnp.zeros((res_in.shape[0], slot_total), jnp.float32)
    outgoing = jnp.take(tokens_t, row_index, axis=1) * live_mask[None, :]
    incoming = lax.all_to_all(outgoing, "dp", split_axis=1, concat_axis=1, tiled=True)
    shard_rows = lax.all_gather(incoming, "expert", axis=0, tiled=True)

    def up_add_block(j, running):
        block_cols = lax.dynamic_slice_in_dim(shard_rows, j * BLOCK, BLOCK, 1)
        product = lax.cond(
            hot_flags[j] > 0,
            lambda: jnp.dot(hot_in, block_cols, preferred_element_type=jnp.float32),
            lambda: jnp.dot(res_in, block_cols, preferred_element_type=jnp.float32),
        )
        previous = lax.dynamic_slice_in_dim(running, j * BLOCK, BLOCK, 1)
        return lax.dynamic_update_slice_in_dim(running, previous + product, j * BLOCK, 1)

    gate_up = lax.fori_loop(0, num_blocks, up_add_block, empty_sum)
    half_rows = gate_up.shape[0] // 2
    hidden = (jax.nn.silu(gate_up[:half_rows]) * gate_up[half_rows:]).astype(jnp.bfloat16)
    res_moved, hot_moved = (
        lax.all_to_all(w_out, "expert", split_axis=1, concat_axis=2, tiled=True),
        lax.all_to_all(hot_out_full, "expert", split_axis=1, concat_axis=2, tiled=True),
    )
    res_by_feat = res_moved[0]
    hot_by_feat = hot_moved[0]
    start_sum = jnp.zeros((feature_rows, slot_total), jnp.float32)
    piece = lax.all_gather(hidden, "expert", axis=0, tiled=True)
    count_rows = piece.shape[0]
    groups = count_rows // half_rows
    fold_res_cols = res_by_feat.reshape(feature_rows, groups, half_rows)
    fold_hot_cols = hot_by_feat.reshape(feature_rows, groups, half_rows)

    def fold_add_block(j, running):
        hidden_block = lax.dynamic_slice_in_dim(piece, j * BLOCK, BLOCK, 1).reshape(
            groups, half_rows, BLOCK
        )
        sums = lax.cond(
            hot_flags[j] > 0,
            lambda: jnp.einsum(
                "dgf,gfb->gdb", fold_hot_cols, hidden_block, preferred_element_type=jnp.float32
            ),
            lambda: jnp.einsum(
                "dgf,gfb->gdb", fold_res_cols, hidden_block, preferred_element_type=jnp.float32
            ),
        )
        rounded = jnp.sum(sums.astype(jnp.bfloat16).astype(jnp.float32), axis=0)
        previous = lax.dynamic_slice_in_dim(running, j * BLOCK, BLOCK, 1)
        return lax.dynamic_update_slice_in_dim(running, previous + rounded, j * BLOCK, 1)

    summed = lax.fori_loop(0, num_blocks, fold_add_block, start_sum)
    expert_out = summed.astype(jnp.bfloat16)
    returned = lax.all_to_all(expert_out, "dp", split_axis=1, concat_axis=1, tiled=True)
    choose = (slot_ids[:, None] == jnp.arange(tok_local, dtype=jnp.int32)[None, :]).astype(
        jnp.float32
    )
    choose = choose * slot_weights[:, None]
    choose_high = choose.astype(jnp.bfloat16)
    choose_low = (choose - choose_high.astype(jnp.float32)).astype(jnp.bfloat16)
    mixed = jnp.dot(returned, choose_high, preferred_element_type=jnp.float32)
    mixed = mixed + jnp.dot(returned, choose_low, preferred_element_type=jnp.float32)
    return mixed.astype(jnp.bfloat16)


def solution(mesh):
    return jax.shard_map(
        local,
        mesh=mesh,
        in_specs=(
            P("expert", "dp"),
            P("dp", None),
            P("dp", None),
            P("dp", None),
            P(),
            P("dp", None, "expert", None),
            P("dp", None, "expert"),
        ),
        out_specs=P("expert", "dp"),
        check_vma=False,
    )
```

profile of v0, /device:TPU:0, one launch (start us, length us, event | category | flops | bytes accessed | tf_op | source)
XLA Modules:
  0.0 689.5 jit_solution(4974403470930709530)
XLA Ops:
  8.1 11.9 %fusion.13 = (bf16[1,7168,256]{2,0,1:T(2,128)(2,1)}, bf16[1,7168,256]{2,0,1:T(2,128)(2,1)}) fusion(bf16[1,7168,256]{2,1,0:T(8,128)(2,1)} %param.21, pred[]{:T(512)S(6)} %eq.10), kind=kLoop, calls=%fused_computation.31 | loop fusion | flops 1835008 | bytes 11010049 | tf_op args[6]
  20.0 3.4 broadcast_select_fusion.1
  24.6 4.0 gather_fusion
  29.1 47.0 %all_to_all.51 = bf16[896,4,256]{0,2,1:T(8,128)(2,1)S(1)} all-to-all(bf16[896,4,256]{0,2,1:T(8,128)(2,1)S(1)} %select_multiply_fusion), channel_id=1, replica_groups=mesh['expert'=8,'dp'=4] {'dp'}, dimensions={1} | all-to-all | bytes 3670016 | tf_op jit(solution)/shard_map/all_to_all | solution.py:32
  79.1 38.4 %reduce.4 = bf16[7168,256]{1,0:T(8,128)(2,1)} reduce(bf16[7168,1,256]{2,1,0:T(2,128)(2,1)} %bitcast.54, bf16[]{:T(256)} %broadcast.60), dimensions={1}, to_apply=%bitcast.26.reduce_sub_computation | reduce | bytes 7340034
  117.5 6.8 reshape.71
  124.3 5.9 all-to-all-start.1
  130.4 170.1 %all-reduce.3.cloned.1.call-done = (bf16[512,7168]{1,0:T(8,128)(2,1)}, bf16[1,7168,256]{2,0,1:T(2,128)(2,1)}) async-done(((bf16[512,7168]{1,0:T(8,128)(2,1)}, bf16[1,7168,256]{2,0,1:T(2,128)(2,1)}), (bf16[512,7168]{1,0:T(8,128)(2,1)}, bf16[1,7168,256]{2,0,1:T(2,128)(2,1)})) %all-reduce.3.cloned.1.call-update) | async-done | bytes 11010064 | tf_op jit(solution)/shard_map/psum | solution.py:11
  300.6 49.0 %all-gather.3.cloned.1.call-done = bf16[7168,1024]{1,0:T(8,128)(2,1)} async-done(((bf16[896,1024]{1,0:T(8,128)(2,1)}), bf16[7168,1024]{1,0:T(8,128)(2,1)}) %all-gather.3.cloned.1.call-update) | async-done | bytes 14680080 | tf_op jit(solution)/shard_map/all_gather | solution.py:33
  349.8 65.3 %while.26 = (s32[]{:T(128)}, f32[512,1024]{1,0:T(8,128)S(1)}, s32[8]{0:T(128)S(1)}, bf16[7168,1024]{1,0:T(8,128)(2,1)}, bf16[512,7168]{1,0:T(8,128)(2,1)}, /*ind...) while((s32[]{:T(128)}, f32[512,1024]{1,0:T(8,128)S(1)}, ...), condition=%wide.region_4.5_spmd, body=%wide.region_1.4_spmd.sunk | while | flops 939589632 | bytes 13893861 | solution.py:45
  352.7 5.2 conditional.4
  352.7 5.2 fusion.14
  360.8 5.2 conditional.4
  360.9 5.2 fusion.15
  369.0 5.2 conditional.4
  369.0 5.2 fusion.14
  377.2 5.2 conditional.4
  377.2 5.2 fusion.15
  385.3 5.2 conditional.4
  385.4 5.2 fusion.14
  393.5 5.2 conditional.4
  393.5 5.2 fusion.14
  401.7 5.2 conditional.4
  401.7 5.2 fusion.15
  409.8 5.2 conditional.4
  409.8 5.2 fusion.14
  416.2 38.3 %reduce.5 = bf16[7168,256]{1,0:T(8,128)(2,1)} reduce(bf16[7168,1,256]{2,1,0:T(2,128)(2,1)} %bitcast.60, bf16[]{:T(256)} %broadcast.60), dimensions={1}, to_apply=%bitcast.28.reduce_sub_computation | reduce | bytes 7340034
  454.5 6.7 reshape.73
  461.2 4.7 all-to-all-start.2
  465.9 8.3 %reshape.72 = bf16[7168,1,256]{2,1,0:T(2,128)(2,1)} reshape(bf16[8,2,114688]{2,1,0:T(2,128)(2,1)} %all-to-all-done.1) | data formatting | bytes 7340032
  474.2 5.6 copy.25
  479.8 83.8 %all-to-all-done.2 = bf16[8,2,114688]{2,1,0:T(2,128)(2,1)} async-done(((bf16[8,2,114688]{2,1,0:T(2,128)(2,1)}), bf16[8,2,114688]{2,1,0:T(2,128)(2,1)}, u32[]{:S(2)}, u32[]{:S(2)}) %all-to-all-start.2) | async-done | bytes 3670048 | tf_op jit(solution)/shard_map/all_to_all | solution.py:50
  563.6 8.3 %reshape.74 = bf16[7168,1,256]{2,1,0:T(2,128)(2,1)} reshape(bf16[8,2,114688]{2,1,0:T(2,128)(2,1)} %all-to-all-done.2) | data formatting | bytes 7340032
  571.8 5.5 copy.26
  579.4 64.8 %while.27 = (s32[]{:T(128)}, f32[896,1024]{0,1:T(8,128)}, s32[8]{0:T(128)S(1)}, bf16[2048,1024]{1,0:T(8,128)(2,1)}, bf16[896,8,256]{2,0,1:T(8,128)(2,1)}, /*inde...) while((s32[]{:T(128)}, f32[896,1024]{0,1:T(8,128)}, ...), condition=%wide.region_10.11_spmd, body=%wide.region_6.10_spmd.sunk | while | flops 471597056 | bytes 14418153 | solution.py:78
  581.7 3.2 conditional.5
  581.7 3.2 fusion.16
  589.8 3.2 conditional.5
  589.8 3.2 fusion.17
  597.9 3.2 conditional.5
  597.9 3.2 fusion.16
  606.0 3.2 conditional.5
  614.1 3.2 conditional.5
  622.2 3.2 conditional.5
  630.3 3.2 conditional.5
  638.4 3.2 conditional.5
  644.2 3.5 convert_element_type.60
  650.4 26.1 %all_to_all.52 = bf16[896,4,256]{2,0,1:T(8,128)(2,1)} all-to-all(bf16[896,4,256]{2,0,1:T(8,128)(2,1)S(1)} %copy.19), channel_id=1, replica_groups=mesh['expert'=8,'dp'=4] {'dp'}, dimensions={1} | all-to-all | bytes 3670016 | tf_op jit(solution)/shard_map/all_to_all | solution.py:80
  (128 shorter events, 84.7 us)
Async XLA Ops:
  7.4 293.2 %all-reduce.3.cloned.1.call-start = ((), (), s32[]{:S(2)}) async-start(), calls=%async_computation.6 | async-start | bytes 29360128 | tf_op jit(solution)/shard_map/psum | solution.py:11
  8.0 11.9 %copy-start = (bf16[1,2,256,7168]{3,2,1,0:T(8,128)(2,1)S(1)}, bf16[1,2,256,7168]{3,2,1,0:T(8,128)(2,1)}, u32[]{:S(2)}) copy-start(bf16[1,2,256,7168]{3,2,1,0:T(8,128)(2,1)} %param.20) | copy-start | bytes 22020100
  23.4 0.9 copy-start.1
  23.4 1.1 copy-start.2
  23.4 326.1 %all-gather.3.cloned.1.call-start = ((), (), s32[]{:S(2)}) async-start(), calls=%async_computation.4 | async-start | bytes 16515072 | tf_op jit(solution)/shard_map/all_gather | solution.py:33
  124.2 225.5 %copy-start.4 = (s32[1,8]{1,0:T(1,128)S(1)}, s32[1,8]{1,0:T(1,128)}, u32[]{:S(2)}) copy-start(s32[1,8]{1,0:T(1,128)} %param.18) | copy-start | bytes 100
  124.3 337.0 %all-to-all-start.1 = ((bf16[8,2,114688]{2,1,0:T(2,128)(2,1)}), bf16[8,2,114688]{2,1,0:T(2,128)(2,1)}, u32[]{:S(2)}, u32[]{:S(2)}) async-start(bf16[8,2,114688]{2,1,0:T(2,128)(2,1)} %reshape.71), calls=%async_computation.1 | async-start | bytes 7340032 | tf_op jit(solution)/shard_map/all_to_all | solution.py:49
  130.2 447.1 %all-gather.5.cloned.1.call-start = ((), (), s32[]{:S(2)}) async-start(), calls=%async_computation.5 | async-start | bytes 4718592 | tf_op jit(solution)/shard_map/all_gather | solution.py:55
  461.2 102.3 %all-to-all-start.2 = ((bf16[8,2,114688]{2,1,0:T(2,128)(2,1)}), bf16[8,2,114688]{2,1,0:T(2,128)(2,1)}, u32[]{:S(2)}, u32[]{:S(2)}) async-start(bf16[8,2,114688]{2,1,0:T(2,128)(2,1)} %reshape.73), calls=%async_computation.2 | async-start | bytes 7340032 | tf_op jit(solution)/shard_map/all_to_all | solution.py:50
  650.4 28.9 %copy-start.3 = (f32[1,1024]{1,0:T(1,128)S(1)}, f32[1,1024]{1,0:T(1,128)}, u32[]{:S(2)}) copy-start(f32[1,1024]{1,0:T(1,128)} %param.17) | copy-start | bytes 12292
Sparse Core Ops, SparseCore 0:
  23.6 276.9 all-reduce.2
Sparse Core Ops, SparseCore 1:
  78.6 270.8 all-gather.2
  416.3 97.5 all-gather.4
where the time goes:
time: 692 us; the launch traced here: 689 us
  waiting for transfers between devices  303 us (44%)
  local copies, waits for them, and re-layouts  106 us (15%)
  other arithmetic  100 us (14%)
  blocking collectives  73 us (11%)
  matrix products  69.2 us (10%)
  between operations  15.7 us (2%)
  loops' own time  11.2 us (2%)
  starting transfers between devices  10.9 us (2%)
    psum x1, waiting for transfers between devices, from_root(): return lax.psum(kept, axis)  170 us
    unnamed x3, other arithmetic  88.7 us
    all_to_all x1, waiting for transfers between devices, local(): lax.all_to_all(hot_out_full, 'expert', split_axis=1, concat_axis=2, tiled...  83.8 us
    all_gather x1, waiting for transfers between devices, local(): shard_rows = lax.all_gather(incoming, 'expert', axis=0, tiled=True)  49 us
    all_to_all x1, blocking collectives, local(): lax.all_to_all(outgoing, 'dp', split_axis=1, concat_axis=1, tiled=True)  47 us
    unnamed x18, local copies, waits for them, and re-layouts  42.6 us
    all_to_all x1, blocking collectives, local(): lax.all_to_all(expert_out, 'dp', split_axis=1, concat_axis=1, tiled=True)  26.1 us
    dot_general x5, matrix products, up_add_block(): jnp.dot(res_in, block_cols, preferred_element_type=jnp.float32)  25.8 us
  transfers between devices with their start and end apart: 5, of which 3 were waited for; matrix products, arithmetic and copies ran while one was open for 27% of the time, Pallas kernels for 0%

commit v1 on v0

--- a/solution.py
+++ b/solution.py
@@ -8,7 +8,7 @@
 
 def from_root(value, axis, source):
     kept = jnp.where(lax.axis_index(axis) == source, value, 0).astype(value.dtype)
-    return lax.psum(kept, axis)
+    return jnp.sum(lax.all_gather(kept, axis), axis=0)
 
 
 def local(tokens_t, slot_row, slot_gate, block_hot, hot_owner, w_in, w_out):

time: 692 us -> 785 us (1.13)
  waiting for transfers between devices: 303 us -> 367 us
  other arithmetic: 100 us -> 117 us
  local copies, waits for them, and re-layouts: 106 us -> 123 us
    psum x1 -> x0, waiting for transfers between devices: 170 us -> none  [from_root(): return lax.psum(kept, axis)]
    all_gather x1, waiting for transfers between devices: 49 us -> 189 us  [local(): shard_rows = lax.all_gather(incoming, 'expert', axis=0, tiled=True)]
    all_gather x0 -> x2, waiting for transfers between devices: none -> 108 us  [from_root(): return jnp.sum(lax.all_gather(kept, axis), axis=0)]
    reduce_sum x0 -> x2, other arithmetic: none -> 26.1 us  [from_root(): return jnp.sum(lax.all_gather(kept, axis), axis=0)]
    all_to_all x1, waiting for transfers between devices: 83.8 us -> 70.6 us  [local(): lax.all_to_all(hot_out_full, 'expert', split_axis=1, concat_axis=2, tiled...]
    unnamed x3 -> x2, other arithmetic: 88.7 us -> 76.8 us
    unnamed x18 -> x17, local copies, waits for them, and re-layouts: 42.6 us -> 50.3 us
  transfers between devices with their start and end apart: 5 -> 6, of which waited for: 3 -> 4; matrix products, arithmetic and copies ran while one was open for 27% -> 30% of each run, Pallas kernels for 0% -> 0%
where the time goes in v1:
time: 785 us; the launch traced here: 782 us
  waiting for transfers between devices  367 us (47%)
  local copies, waits for them, and re-layouts  123 us (16%)
  other arithmetic  117 us (15%)
  matrix products  71.6 us (9%)
  blocking collectives  67.7 us (9%)
  between operations  13.9 us (2%)
  starting transfers between devices  12 us (2%)
  loops' own time  11 us (1%)
    all_gather x1, waiting for transfers between devices, local(): shard_rows = lax.all_gather(incoming, 'expert', axis=0, tiled=True)  189 us
    all_gather x2, waiting for transfers between devices, from_root(): return jnp.sum(lax.all_gather(kept, axis), axis=0)  108 us
    unnamed x2, other arithmetic  76.8 us
    all_to_all x1, waiting for transfers between devices, local(): lax.all_to_all(hot_out_full, 'expert', split_axis=1, concat_axis=2, tiled...  70.6 us
    unnamed x17, local copies, waits for them, and re-layouts  50.3 us
    all_to_all x1, blocking collectives, local(): lax.all_to_all(outgoing, 'dp', split_axis=1, concat_axis=1, tiled=True)  41.6 us
    dot_general x5, matrix products, up_add_block(): jnp.dot(res_in, block_cols, preferred_element_type=jnp.float32)  26.4 us
    reduce_sum x2, other arithmetic, from_root(): return jnp.sum(lax.all_gather(kept, axis), axis=0)  26.1 us
  transfers between devices with their start and end apart: 6, of which 4 were waited for; matrix products, arithmetic and copies ran while one was open for 30% of the time, Pallas kernels for 0%

profile of v1, /device:TPU:0, one launch (start us, length us, event | category | flops | bytes accessed | tf_op | source)
XLA Modules:
  0.0 782.4 jit_solution(11277506216955260645)
XLA Ops:
  7.2 3.4 broadcast_select_fusion
  11.9 4.0 gather_fusion
  16.3 41.6 %all_to_all.51 = bf16[896,4,256]{0,2,1:T(8,128)(2,1)S(1)} all-to-all(bf16[896,4,256]{0,2,1:T(8,128)(2,1)S(1)} %select_multiply_fusion), channel_id=1, replica_groups=mesh['expert'=8,'dp'=4] {'dp'}, dimensions={1} | all-to-all | bytes 3670016 | tf_op jit(solution)/shard_map/all_to_all | solution.py:32
  62.6 7.7 copy.29
  70.8 38.5 %reduce.12 = bf16[7168,256]{1,0:T(8,128)(2,1)} reduce(bf16[7168,1,256]{2,1,0:T(2,128)(2,1)} %bitcast.58, bf16[]{:T(256)} %broadcast.60), dimensions={1}, to_apply=%bitcast.44.reduce_sub_computation | reduce | bytes 7340034
  109.3 6.7 reshape.78
  116.0 6.2 all-to-all-start.1
  122.3 83.4 %all-gather.11.cloned.1.call-done = bf16[4,2,256,7168]{3,2,1,0:T(8,128)(2,1)} async-done(((bf16[1,2,256,7168]{3,2,1,0:T(8,128)(2,1)}), bf16[4,2,256,7168]{3,2,1,0:T(8,128)(2,1)}) %all-gather.11.cloned.1.call-update) | async-done | bytes 29360144 | tf_op jit(solution)/shard_map/all_gather | solution.py:11
  205.8 15.4 %reduce.4 = bf16[2,256,7168]{2,1,0:T(8,128)(2,1)} reduce(bf16[4,2,256,7168]{3,2,1,0:T(8,128)(2,1)} %all-gather.11.cloned.1.call-done, bf16[]{:T(256)} %constant.123.clone.1), dimensions={0}, to_apply=%region_0.1 | reduce | flops 11010048 | bytes 36700160 | tf_op jit(solution)/shard_map/reduce_sum | solution.py:11
  221.2 188.8 %all-gather.7.cloned.1.call-done = bf16[7168,1024]{1,0:T(8,128)(2,1)} async-done(((bf16[896,1024]{1,0:T(8,128)(2,1)}), bf16[7168,1024]{1,0:T(8,128)(2,1)}) %all-gather.7.cloned.1.call-update) | async-done | bytes 14680080 | tf_op jit(solution)/shard_map/all_gather | solution.py:33
  410.2 68.1 %while.26 = (s32[]{:T(128)}, f32[512,1024]{1,0:T(8,128)S(1)}, s32[8]{0:T(128)S(1)}, bf16[7168,1024]{1,0:T(8,128)(2,1)}, bf16[512,7168]{1,0:T(8,128)(2,1)}, /*ind...) while((s32[]{:T(128)}, f32[512,1024]{1,0:T(8,128)S(1)}, ...), condition=%wide.region_4.5_spmd, body=%wide.region_1.4_spmd.sunk | while | flops 939589632 | bytes 13893861 | solution.py:45
  413.1 5.5 conditional.4
  413.1 5.5 fusion.13
  422.0 7.0 conditional.4
  422.0 7.0 fusion.14
  432.0 5.3 conditional.4
  432.0 5.3 fusion.13
  440.3 5.2 conditional.4
  440.3 5.2 fusion.14
  448.5 5.2 conditional.4
  448.5 5.2 fusion.13
  456.7 5.2 conditional.4
  456.7 5.2 fusion.13
  464.8 5.2 conditional.4
  464.8 5.2 fusion.14
  473.0 5.3 conditional.4
  473.0 5.3 fusion.13
  479.5 24.3 %all-gather.13.cloned.1.call-done = bf16[4,7168,256]{2,1,0:T(8,128)(2,1)} async-done(((bf16[1,7168,256]{2,1,0:T(8,128)(2,1)}), bf16[4,7168,256]{2,1,0:T(8,128)(2,1)}) %all-gather.13.cloned.1.call-update) | async-done | bytes 14680080 | tf_op jit(solution)/shard_map/all_gather | solution.py:11
  503.8 10.7 %reduce.5 = bf16[7168,256]{1,0:T(8,128)(2,1)} reduce(bf16[4,7168,256]{2,1,0:T(8,128)(2,1)} %all-gather.13.cloned.1.call-done, bf16[]{:T(256)} %constant.123.clone.1), dimensions={0}, to_apply=%region_5.6 | reduce | flops 5505024 | bytes 18350082 | tf_op jit(solution)/shard_map/reduce_sum | solution.py:11
  514.5 7.8 copy.28
  522.2 38.4 %reduce.13 = bf16[7168,256]{1,0:T(8,128)(2,1)} reduce(bf16[7168,1,256]{2,1,0:T(2,128)(2,1)} %bitcast.59, bf16[]{:T(256)} %broadcast.60), dimensions={1}, to_apply=%bitcast.43.reduce_sub_computation | reduce | bytes 7340034
  560.6 6.7 reshape.80
  567.3 5.5 all-to-all-start.2
  572.8 8.3 %reshape.79 = bf16[7168,1,256]{2,1,0:T(2,128)(2,1)} reshape(bf16[8,2,114688]{2,1,0:T(2,128)(2,1)} %all-to-all-done.1) | data formatting | bytes 7340032
  581.1 5.6 copy.24
  586.7 70.6 %all-to-all-done.2 = bf16[8,2,114688]{2,1,0:T(2,128)(2,1)} async-done(((bf16[8,2,114688]{2,1,0:T(2,128)(2,1)}), bf16[8,2,114688]{2,1,0:T(2,128)(2,1)}, u32[]{:S(2)}, u32[]{:S(2)}) %all-to-all-start.2) | async-done | bytes 3670048 | tf_op jit(solution)/shard_map/all_to_all | solution.py:50
  657.2 8.3 %reshape.81 = bf16[7168,1,256]{2,1,0:T(2,128)(2,1)} reshape(bf16[8,2,114688]{2,1,0:T(2,128)(2,1)} %all-to-all-done.2) | data formatting | bytes 7340032
  665.5 5.5 copy.25
  673.0 64.9 %while.27 = (s32[]{:T(128)}, f32[896,1024]{0,1:T(8,128)}, s32[8]{0:T(128)S(1)}, bf16[2048,1024]{1,0:T(8,128)(2,1)}, bf16[896,8,256]{2,0,1:T(8,128)(2,1)}, /*inde...) while((s32[]{:T(128)}, f32[896,1024]{0,1:T(8,128)}, ...), condition=%wide.region_10.11_spmd, body=%wide.region_6.10_spmd.sunk | while | flops 471597056 | bytes 14418153 | solution.py:78
  675.4 3.2 conditional.5
  683.5 3.2 conditional.5
  691.6 3.2 conditional.5
  699.7 3.2 conditional.5
  707.8 3.2 conditional.5
  716.0 3.2 conditional.5
  724.1 3.2 conditional.5
  738.0 3.5 convert_element_type.64
  744.2 26.1 %all_to_all.52 = bf16[896,4,256]{2,0,1:T(8,128)(2,1)} all-to-all(bf16[896,4,256]{2,0,1:T(8,128)(2,1)S(1)} %copy.18), channel_id=1, replica_groups=mesh['expert'=8,'dp'=4] {'dp'}, dimensions={1} | all-to-all | bytes 3670016 | tf_op jit(solution)/shard_map/all_to_all | solution.py:80
  (133 shorter events, 100.1 us)
Async XLA Ops:
  6.5 199.2 %all-gather.11.cloned.1.call-start = ((), (), s32[]{:S(2)}) async-start(), calls=%async_computation.6 | async-start | bytes 36700160 | tf_op jit(solution)/shard_map/all_gather | solution.py:11
  10.7 0.9 copy-start
  10.7 1.1 copy-start.1
  10.7 399.3 %all-gather.7.cloned.1.call-start = ((), (), s32[]{:S(2)}) async-start(), calls=%async_computation.4 | async-start | bytes 16515072 | tf_op jit(solution)/shard_map/all_gather | solution.py:33
  60.4 443.3 %all-gather.13.cloned.1.call-start = ((), (), s32[]{:S(2)}) async-start(), calls=%async_computation.7 | async-start | bytes 18350080 | tf_op jit(solution)/shard_map/all_gather | solution.py:11
  116.0 451.3 %all-to-all-start.1 = ((bf16[8,2,114688]{2,1,0:T(2,128)(2,1)}), bf16[8,2,114688]{2,1,0:T(2,128)(2,1)}, u32[]{:S(2)}, u32[]{:S(2)}) async-start(bf16[8,2,114688]{2,1,0:T(2,128)(2,1)} %reshape.78), calls=%async_computation.1 | async-start | bytes 7340032 | tf_op jit(solution)/shard_map/all_to_all | solution.py:49
  122.1 548.9 %all-gather.9.cloned.1.call-start = ((), (), s32[]{:S(2)}) async-start(), calls=%async_computation.5 | async-start | bytes 4718592 | tf_op jit(solution)/shard_map/all_gather | solution.py:55
  122.3 287.9 %copy-start.3 = (s32[1,8]{1,0:T(1,128)S(1)}, s32[1,8]{1,0:T(1,128)}, u32[]{:S(2)}) copy-start(s32[1,8]{1,0:T(1,128)} %param.18) | copy-start | bytes 100
  567.3 89.9 %all-to-all-start.2 = ((bf16[8,2,114688]{2,1,0:T(2,128)(2,1)}), bf16[8,2,114688]{2,1,0:T(2,128)(2,1)}, u32[]{:S(2)}, u32[]{:S(2)}) async-start(bf16[8,2,114688]{2,1,0:T(2,128)(2,1)} %reshape.80), calls=%async_computation.2 | async-start | bytes 7340032 | tf_op jit(solution)/shard_map/all_to_all | solution.py:50
  744.2 28.9 %copy-start.2 = (f32[1,1024]{1,0:T(1,128)S(1)}, f32[1,1024]{1,0:T(1,128)}, u32[]{:S(2)}) copy-start(f32[1,1024]{1,0:T(1,128)} %param.17) | copy-start | bytes 12292
Sparse Core Ops, SparseCore 0:
  10.8 194.9 all-gather.10
  207.9 201.9 all-gather.6
  411.5 92.1 all-gather.12
  505.7 74.6 all-gather.8
